TPU v7x, 512 devices: a whole 4x8x8 slice. The times are simulated.
512 devices in a mesh: dp: 16 (over z, core), tp: 32 (over y, x).
Axes of the slice: x: 4, y: 8, z: 8, core: 2. Of those that a mesh axis runs over, the one named last changes fastest.
Arguments:
- q_new: bfloat16 [512, 1536], P(('dp', 'tp'))
- new_key_value: bfloat16 [512, 512], P(('dp', 'tp')), may hold values from -6 to 6
- resid_dec: bfloat16 [512, 1536], P(('dp', 'tp')), may hold values from -6 to 6
- placing: int32 [512], replicated, may hold values from 0 to 511, as said below
- lengths: int32 [512], P('dp'), may hold values from 5 to 2048, as said below
- write_pos: int32 [512], P('dp'), may hold values from 4 to 2047, as said below
- k_cache: bfloat16 [512, 2, 2048, 128], P('dp', None, 'tp')
- value_cache: bfloat16 [512, 2, 2048, 128], P('dp', None, 'tp'), may hold values from -6 to 6
- w_out: bfloat16 [1536, 1536], P(None, 'tp'), may hold values from -0.15625 to 0.15625
- x_pre: bfloat16 [32256, 1536], P(('dp', 'tp')), may hold values from -6 to 6
- routes: int32 [32768, 4], P(('dp', 'tp')), may hold values from 0 to 31, all different within a row; in each aligned block of 64 rows (0 to 63, 64 to 127, ...) at most 16 rows name the same one
- route_scale: float32 [32768, 4], P(('dp', 'tp')), may hold values from 0.2 to 2
- moe_gain: float32 [1536], replicated, may hold values from 0.5 to 1.5
- w_gate: bfloat16 [32, 768, 1536], P('tp', 'dp'), may hold values from -0.15625 to 0.15625
- w_up: bfloat16 [32, 768, 1536], P('tp', 'dp'), may hold values from -0.15625 to 0.15625
- w_down: bfloat16 [32, 768, 1536], P('tp', 'dp'), may hold values from -0.21875 to 0.21875
Outputs:
- out_pre: bfloat16 [32256, 1536], P(('dp', 'tp'))
- out_dec: bfloat16 [512, 1536], P(('dp', 'tp'))
Inputs may be any that keep to these rules, and one draw needn't show every extreme that they name: Each of 0 to 511 appears once; cache row j belongs to request placing[j]. `lengths`: a cache row is either full (2048 live slots) or filled from slot 0 up; some row is full. `write_pos`: below the row's length; a row that is not full writes at its length - 1, a full row anywhere past the sink slots. `routes`: the 64 rows of one device name any one expert at most 16 times.
All inputs are finite; a program needn't handle non-finite values.
Results may differ from a plain program's by a relative error of at most 0.007.
Values may be sent and summed in bfloat16 or wider, within the bound.
No kernel may reach another device: no remote copies, remote signals or barrier semaphores. Data moves between devices by JAX's collectives and lax.ppermute only.
A program may use at most 64 MiB of HBM per device.

v0:
```python
import jax
import jax.numpy as jnp
from jax import lax
from jax.sharding import PartitionSpec as P

HIGHEST = lax.Precision.HIGHEST
F32 = jnp.float32
BF16 = jnp.bfloat16


def contract_rows(left_rows, unit_rows):
    return lax.dot_general(
        left_rows, unit_rows, (((1,), (1,)), ((), ())), preferred_element_type=F32
    )


def swap(blocks, axis_name):
    return lax.all_to_all(blocks, axis_name, split_axis=0, concat_axis=0, tiled=True)


def spread(block, axis_name):
    members = lax.axis_size(axis_name)
    return swap(jnp.broadcast_to(block[None], (members,) + block.shape), axis_name)


def choose_rows(table, rows):
    return jnp.dot(table.astype(BF16), rows, preferred_element_type=F32).astype(BF16)


def pieces_of(x):
    high = lax.reduce_precision(x, 8, 7)
    middle = lax.reduce_precision(x - high, 8, 7)
    low = lax.reduce_precision(x - high - middle, 8, 7)
    return (high.astype(BF16), middle.astype(BF16), low.astype(BF16))


def rms(rows_f32, gain):
    mean_square = jnp.mean(rows_f32 * rows_f32, axis=-1, keepdims=True)
    return (rows_f32 * lax.rsqrt(mean_square + 1e-06) * gain).astype(BF16)


def expert_units(rows, units):
    gate = contract_rows(rows, units[0])
    upper = contract_rows(rows, units[1])
    active = (jnp.maximum(gate, 0.0) * upper).astype(BF16)
    return jnp.dot(active, units[2], preferred_element_type=F32).astype(BF16)


def on_device(
    q_new,
    new_key_value,
    resid_dec,
    placing,
    lengths,
    write_pos,
    k_cache,
    value_cache,
    w_out,
    x_pre,
    routes,
    route_scale,
    moe_gain,
    w_gate,
    w_up,
    w_down,
):
    dp_size = lax.axis_size("dp")
    tp_size = lax.axis_size("tp")
    dp_group = lax.axis_index("dp")
    tp_lane = lax.axis_index("tp")
    group_reqs, kv_heads, slot_dev, head_size = k_cache.shape
    width = q_new.shape[1]
    heads = width // head_size
    per_group = heads // kv_heads
    total_reqs = placing.shape[0]
    experts = tp_size * w_gate.shape[0]
    assert group_reqs == tp_size and experts == tp_size
    out_rows = lax.all_gather(w_out.T, "tp", axis=0, tiled=True)
    stacked = jnp.concatenate([w_gate, w_up, w_down], axis=0)
    stacked, _ = lax.optimization_barrier((stacked, out_rows))
    units = lax.all_gather(stacked, "dp", axis=1, tiled=True)
    columns = heads + 2 * kv_heads
    share = tp_size // columns
    chosen_rows = group_reqs // share
    fresh = jnp.concatenate([q_new, new_key_value], axis=1).reshape(1, columns, 1, head_size)
    by_head = swap(
        jnp.broadcast_to(fresh, (share, columns, 1, head_size)).reshape(tp_size, 1, head_size), "tp"
    )
    all_rows = spread(by_head.reshape(tp_size, head_size), "dp").reshape(total_reqs, head_size)
    first_row = dp_group * group_reqs + tp_lane // columns * chosen_rows
    wanted = lax.dynamic_slice_in_dim(placing, first_row, chosen_rows)
    request_ids = jnp.arange(total_reqs, dtype=jnp.int32)
    mine = choose_rows(wanted[:, None] == request_ids[None, :], all_rows)
    heads_here = spread(mine, "tp").reshape(share, columns, chosen_rows, head_size)
    cached = jnp.transpose(heads_here, (0, 2, 1, 3)).reshape(group_reqs, columns, head_size)
    query_head_list = cached[:, :heads].reshape(group_reqs, kv_heads, per_group, head_size)
    incoming_key = cached[:, heads : heads + kv_heads][:, :, None, :]
    incoming_value = cached[:, heads + kv_heads :][:, :, None, :]
    slot_ids = tp_lane * slot_dev + jnp.arange(slot_dev, dtype=jnp.int32)
    written = (slot_ids[None, :] == write_pos[:, None])[:, None, :, None]
    key_rows = jnp.where(written, incoming_key, k_cache)
    value_rows = jnp.where(written, incoming_value, value_cache).astype(F32)
    scores = jnp.einsum(
        "rgqd,rgsd->rgqs", query_head_list, key_rows, preferred_element_type=F32
    ) * head_size ** (-0.5)
    is_valid = (slot_ids[None, :] < lengths[:, None])[:, None, None, :]
    masked = jnp.where(is_valid, scores, -1e30)
    local_peak = jnp.max(masked, axis=-1)
    weights = jnp.where(is_valid, jnp.exp(masked - local_peak[..., None]), 0.0)
    local_total = jnp.sum(weights, axis=-1)
    local_mixed = jnp.einsum("rgqs,rgsd->rgqd", weights, value_rows, precision=HIGHEST)

    def lane_row(values):
        row = jnp.concatenate(pieces_of(values.reshape(group_reqs, heads)), axis=1)
        return jnp.pad(row, ((0, 0), (0, head_size - row.shape[1])))[:, None, :]

    parts = jnp.concatenate(
        [
            local_mixed.reshape(group_reqs, heads, head_size).astype(BF16),
            lane_row(local_peak),
            lane_row(local_total),
            jnp.zeros((group_reqs, 2, head_size), BF16),
        ],
        axis=1,
    )
    gathered = swap(parts, "tp")
    tail = gathered[:, heads : heads + 2, : 3 * heads].astype(F32)
    tail = tail[..., :heads] + tail[..., heads : 2 * heads] + tail[..., 2 * heads :]
    peaks, totals = (tail[:, 0], tail[:, 1])
    scale = jnp.exp(peaks - jnp.max(peaks, axis=0, keepdims=True))
    total = jnp.sum(scale * totals, axis=0)
    mixed = jnp.sum(scale[:, :, None] * gathered[:, :heads].astype(F32), axis=0)
    attention_row = (mixed / total[:, None]).astype(BF16)
    projected = contract_rows(attention_row.reshape(1, width), out_rows).astype(BF16)
    request = lax.dynamic_slice_in_dim(placing, dp_group * group_reqs + tp_lane, 1)[0]
    lane_of = jnp.arange(tp_size, dtype=jnp.int32) == request % tp_size
    no_value = jnp.zeros((), BF16)
    by_lane = swap(
        jnp.where(lane_of[:, None], projected, no_value).reshape(tp_size, heads, head_size), "tp"
    )
    group_rows = lax.dynamic_slice_in_dim(placing, dp_group * group_reqs, group_reqs)
    here = group_rows % tp_size == tp_lane
    to_group = (group_rows // tp_size)[None, :] == jnp.arange(dp_size, dtype=jnp.int32)[:, None]
    outbound = choose_rows(to_group & here[None, :], by_lane.reshape(tp_size, width))
    inbound = swap(outbound.reshape(dp_size, heads, head_size), "dp").reshape(dp_size, width)
    home_ids = dp_group * tp_size + tp_lane
    source = jnp.sum(jnp.where(placing == home_ids, jnp.arange(total_reqs, dtype=jnp.int32), 0))
    source_group = source // group_reqs
    from_group = jnp.arange(dp_size, dtype=jnp.int32)[None, :] == source_group
    proj_home = choose_rows(from_group, inbound)
    hidden_dec = (resid_dec.astype(F32) + proj_home.astype(F32)).astype(BF16)
    route_weight = route_scale / jnp.sum(route_scale, axis=-1, keepdims=True)
    expert_ids = jnp.arange(experts, dtype=jnp.int32)
    hits = routes[:, :, None] == expert_ids[None, None, :]
    weight_of = jnp.sum(jnp.where(hits, route_weight[:, :, None], 0.0), axis=1)
    moe_rows = jnp.concatenate([x_pre, hidden_dec], axis=0)
    rows_dev = moe_rows.shape[0]
    top_count = routes.shape[1]
    capacity = min(2 * rows_dev * top_count // experts, rows_dev)
    routed = jnp.any(hits, axis=1)
    row_ids = jnp.arange(rows_dev, dtype=jnp.int32)
    before = (row_ids[None, :] < row_ids[:, None]).astype(BF16)
    position = jnp.dot(before, routed.astype(BF16), preferred_element_type=F32).astype(jnp.int32)
    slot_ids_e = jnp.arange(capacity, dtype=jnp.int32)
    pick = routed[:, :, None] & (position[:, :, None] == slot_ids_e[None, None, :])
    pick_table = pick.reshape(rows_dev, experts * capacity)
    rows_f32 = moe_rows.astype(F32)
    normed = rms(rows_f32, moe_gain)
    outgoing = lax.dot_general(
        pick_table.astype(BF16), normed, (((0,), (0,)), ((), ())), preferred_element_type=F32
    ).astype(BF16)
    received = swap(outgoing.reshape(experts, capacity, width), "tp")
    expert_out = expert_units(received.reshape(experts * capacity, width), units)
    returned = swap(expert_out.reshape(experts, capacity, width), "tp")
    flat_back = returned.reshape(experts * capacity, width)
    high, middle, low = pieces_of(weight_of)

    def mix(piece):
        table = jnp.where(pick, piece[:, :, None], no_value)
        return jnp.dot(
            table.reshape(rows_dev, experts * capacity), flat_back, preferred_element_type=F32
        )

    moe_out = (rows_f32 + (mix(high) + mix(middle) + mix(low))).astype(BF16)
    return (moe_out[: rows_dev - 1], moe_out[rows_dev - 1 :])


def solution(mesh):
    placed = (
        P(("dp", "tp"), None),
        P(("dp", "tp"), None),
        P(("dp", "tp"), None),
        P(),
        P("dp"),
        P("dp"),
        P("dp", None, "tp", None),
        P("dp", None, "tp", None),
        P(None, "tp"),
        P(("dp", "tp"), None),
        P(("dp", "tp"), None),
        P(("dp", "tp"), None),
        P(),
        P("tp", "dp", None),
        P("tp", "dp", None),
        P("tp", "dp", None),
    )
    return jax.shard_map(
        on_device,
        mesh=mesh,
        in_specs=placed,
        out_specs=(P(("dp", "tp"), None), P(("dp", "tp"), None)),
        check_vma=False,
    )
```

profile of v0, /device:TPU:2, one launch (start us, length us, event | category | flops | bytes accessed | tf_op | source)
XLA Modules:
  0.0 313.3 jit_solution(5747145062844890888)
XLA Ops:
  8.0 2.0 pad_maximum_fusion
  10.0 93.1 %all-gather.3.cloned.1.call-done = bf16[1536,1536]{1,0:T(8,128)(2,1)} async-done(((bf16[48,1536]{1,0:T(8,128)(2,1)}), bf16[1536,1536]{1,0:T(8,128)(2,1)}) %all-gather.3.cloned.1.call-update) | async-done | bytes 4718608 | tf_op jit(solution)/shard_map/all_gather | solution.py:78
  103.1 0.7 maximum_reduce_fusion
  103.9 16.0 %all_to_all.40 = bf16[32,1,128]{2,1,0:T(2,128)(2,1)S(1)} all-to-all(bf16[32,1,128]{2,1,0:T(2,128)(2,1)S(1)} %copy.71), channel_id=1, replica_groups=mesh['dp'=16,'tp'=32] {'tp'}, dimensions={0} | all-to-all | bytes 16384 | tf_op jit(solution)/shard_map/all_to_all | solution.py:18
  120.6 7.5 %all-to-all-start.1 = ((bf16[16,32,128]{2,1,0:T(8,128)(2,1)}), bf16[16,32,128]{2,1,0:T(8,128)(2,1)S(1)}, u32[]{:S(2)}, u32[]{:S(2)}) async-start(bf16[16,32,128]{2,1,0:T(8,128)(2,1)} %broadcast_in_dim.175), calls=%async_computation.1 | async-start | bytes 262144 | tf_op jit(solution)/shard_map/all_to_all | solution.py:18
  128.3 10.4 %all-to-all-done.1 = bf16[16,32,128]{2,1,0:T(8,128)(2,1)S(1)} async-done(((bf16[16,32,128]{2,1,0:T(8,128)(2,1)}), bf16[16,32,128]{2,1,0:T(8,128)(2,1)S(1)}, u32[]{:S(2)}, u32[]{:S(2)}) %all-to-all-start.1) | async-done | bytes 131104 | tf_op jit(solution)/shard_map/all_to_all | solution.py:18
  139.6 5.1 %all-to-all-start.2 = ((bf16[32,16,128]{2,1,0:T(8,128)(2,1)}), bf16[32,16,128]{2,1,0:T(8,128)(2,1)S(1)}, u32[]{:S(2)}, u32[]{:S(2)}) async-start(bf16[32,16,128]{2,1,0:T(8,128)(2,1)} %broadcast_in_dim.176), calls=%async_computation.2 | async-start | bytes 262144 | tf_op jit(solution)/shard_map/all_to_all | solution.py:18
  147.4 6.6 %all-to-all-done.2 = bf16[32,16,128]{2,1,0:T(8,128)(2,1)S(1)} async-done(((bf16[32,16,128]{2,1,0:T(8,128)(2,1)}), bf16[32,16,128]{2,1,0:T(8,128)(2,1)S(1)}, u32[]{:S(2)}, u32[]{:S(2)}) %all-to-all-start.2) | async-done | bytes 131104 | tf_op jit(solution)/shard_map/all_to_all | solution.py:18
  154.2 1.1 fusion.76
  155.4 1.3 convolution_convert_fusion.3
  157.4 0.7 copy.80
  158.1 5.7 %all-to-all-start.3 = ((bf16[32,16,128]{2,1,0:T(8,128)(2,1)}), bf16[32,16,128]{2,1,0:T(8,128)(2,1)S(1)}, u32[]{:S(2)}, u32[]{:S(2)}) async-start(bf16[32,16,128]{2,1,0:T(8,128)(2,1)} %copy.80), calls=%async_computation.3 | async-start | bytes 262144 | tf_op jit(solution)/shard_map/all_to_all | solution.py:18
  164.0 8.8 %all-to-all-done.3 = bf16[32,16,128]{2,1,0:T(8,128)(2,1)S(1)} async-done(((bf16[32,16,128]{2,1,0:T(8,128)(2,1)}), bf16[32,16,128]{2,1,0:T(8,128)(2,1)S(1)}, u32[]{:S(2)}, u32[]{:S(2)}) %all-to-all-start.3) | async-done | bytes 131104 | tf_op jit(solution)/shard_map/all_to_all | solution.py:18
  173.4 3.7 %convolution_reduce_fusion.1 = bf16[1536]{0:T(1024)(128)(2,1)S(1)} fusion(bf16[1536,1]{0,1:T(2,128)(2,1)S(1)} %reshape.225, bf16[1536,1536]{1,0:T(8,128)(2,1)} %all-gather.3.cloned.1.call-done), kind=kOutput, calls=%fused_computation.21 | convolution fusion | flops 4718592 | bytes 4724736 | tf_op jit(solution)/shard_map/dot_general | solution.py:12
  177.1 0.8 broadcast_select_fusion
  177.9 5.4 %all-to-all-start.4 = ((bf16[32,12,128]{2,1,0:T(8,128)(2,1)}), bf16[32,12,128]{2,1,0:T(8,128)(2,1)S(1)}, u32[]{:S(2)}, u32[]{:S(2)}) async-start(bf16[32,12,128]{2,1,0:T(8,128)(2,1)} %broadcast_select_fusion), calls=%async_computation.4 | async-start | bytes 262144 | tf_op jit(solution)/shard_map/all_to_all | solution.py:18
  183.4 8.9 %all-to-all-done.4 = bf16[32,12,128]{2,1,0:T(8,128)(2,1)S(1)} async-done(((bf16[32,12,128]{2,1,0:T(8,128)(2,1)}), bf16[32,12,128]{2,1,0:T(8,128)(2,1)S(1)}, u32[]{:S(2)}, u32[]{:S(2)}) %all-to-all-start.4) | async-done | bytes 98336 | tf_op jit(solution)/shard_map/all_to_all | solution.py:18
  193.1 3.5 %all-to-all-start.5 = ((bf16[16,12,128]{2,1,0:T(8,128)(2,1)}), bf16[16,12,128]{2,1,0:T(8,128)(2,1)S(1)}, u32[]{:S(2)}, u32[]{:S(2)}) async-start(bf16[16,12,128]{2,1,0:T(8,128)(2,1)} %reshape.219), calls=%async_computation.5 | async-start | bytes 131072 | tf_op jit(solution)/shard_map/all_to_all | solution.py:18
  200.1 4.3 %all-to-all-done.5 = bf16[16,12,128]{2,1,0:T(8,128)(2,1)S(1)} async-done(((bf16[16,12,128]{2,1,0:T(8,128)(2,1)}), bf16[16,12,128]{2,1,0:T(8,128)(2,1)S(1)}, u32[]{:S(2)}, u32[]{:S(2)}) %all-to-all-start.5) | async-done | bytes 49184 | tf_op jit(solution)/shard_map/all_to_all | solution.py:18
  205.4 44.8 %all_to_all.41 = bf16[32,16,1536]{2,1,0:T(8,128)(2,1)S(1)} all-to-all(bf16[32,16,1536]{2,1,0:T(8,128)(2,1)S(1)} %bitcast.91), channel_id=1, replica_groups=mesh['dp'=16,'tp'=32] {'tp'}, dimensions={0} | all-to-all | bytes 3145728 | tf_op jit(solution)/shard_map/all_to_all | solution.py:18
  250.2 3.1 fusion
  253.3 6.8 %convolution_convert_fusion = bf16[512,1536]{1,0:T(8,128)(2,1)} fusion(bf16[3,768,1536]{2,1,0:T(8,128)(2,1)} %all-gather.5.cloned.1.call-done, f32[512,768]{1,0:T(8,128)S(1)} %fusion, bf16[512,1536]{1,0:T(8,128)(2,1)S(1)} %bitcast.93), kind=kOutput, calls=%fused_computation | convolution fusion | flops 2417885184 | bytes 9437184 | tf_op jit(solution)/shard_map/dot_general | solution.py:46
  260.0 5.7 %all-to-all-start.7 = ((bf16[32,16,1536]{2,1,0:T(8,128)(2,1)}), bf16[32,16,1536]{2,1,0:T(8,128)(2,1)S(1)}, u32[]{:S(2)}, u32[]{:S(2)}) async-start(bf16[32,16,1536]{2,1,0:T(8,128)(2,1)} %bitcast.24), calls=%async_computation.7 | async-start | bytes 3145728 | tf_op jit(solution)/shard_map/all_to_all | solution.py:18
  265.8 38.6 %all-to-all-done.7 = bf16[32,16,1536]{2,1,0:T(8,128)(2,1)S(1)} async-done(((bf16[32,16,1536]{2,1,0:T(8,128)(2,1)}), bf16[32,16,1536]{2,1,0:T(8,128)(2,1)S(1)}, u32[]{:S(2)}, u32[]{:S(2)}) %all-to-all-start.7) | async-done | bytes 1572896 | tf_op jit(solution)/shard_map/all_to_all | solution.py:18
  (89 shorter events, 9.6 us)
Async XLA Ops:
  7.2 121.0 %copy-start.6 = (s32[512]{0:T(512)S(1)}, s32[512]{0:T(512)}, u32[]{:S(2)}) copy-start(s32[512]{0:T(512)} %param.19) | copy-start | bytes 6148
  7.2 121.1 %copy-start.3 = (s32[64,4]{0,1:T(4,128)S(1)}, s32[64,4]{0,1:T(4,128)}, u32[]{:S(2)}) copy-start(s32[64,4]{0,1:T(4,128)} %param.26) | copy-start | bytes 3076
  7.2 140.2 %copy-start.7 = (s32[32]{0:T(128)S(1)}, s32[32]{0:T(128)}, u32[]{:S(2)}) copy-start(s32[32]{0:T(128)} %param.20) | copy-start | bytes 388
  7.2 140.2 %copy-start.8 = (s32[32]{0:T(128)S(1)}, s32[32]{0:T(128)}, u32[]{:S(2)}) copy-start(s32[32]{0:T(128)} %param.21) | copy-start | bytes 388
  7.2 95.9 %all-gather.3.cloned.1.call-start = ((), (), s32[]{:S(2)}) async-start(), calls=%async_computation.8 | async-start | bytes 4866048 | tf_op jit(solution)/shard_map/all_gather | solution.py:78
  7.9 146.2 %copy-start.9 = (bf16[32,2,64,128]{3,2,1,0:T(8,128)(2,1)S(1)}, bf16[32,2,64,128]{3,2,1,0:T(8,128)(2,1)}, u32[]{:S(2)}) copy-start(bf16[32,2,64,128]{3,2,1,0:T(8,128)(2,1)} %param.22) | copy-start | bytes 3145732
  8.0 242.2 %all-gather.5.cloned.1.call-start = ((), (), s32[]{:S(2)}) async-start(), calls=%async_computation.9 | async-start | bytes 7520256 | tf_op jit(solution)/shard_map/all_gather | solution.py:81
  120.6 18.1 %all-to-all-start.1 = ((bf16[16,32,128]{2,1,0:T(8,128)(2,1)}), bf16[16,32,128]{2,1,0:T(8,128)(2,1)S(1)}, u32[]{:S(2)}, u32[]{:S(2)}) async-start(bf16[16,32,128]{2,1,0:T(8,128)(2,1)} %broadcast_in_dim.175), calls=%async_computation.1 | async-start | bytes 262144 | tf_op jit(solution)/shard_map/all_to_all | solution.py:18
  138.9 16.5 %copy-start.10 = (bf16[32,2,64,128]{3,2,1,0:T(8,128)(2,1)S(1)}, bf16[32,2,64,128]{3,2,1,0:T(8,128)(2,1)}, u32[]{:S(2)}) copy-start(bf16[32,2,64,128]{3,2,1,0:T(8,128)(2,1)} %param.23) | copy-start | bytes 3145732
  139.6 14.5 %all-to-all-start.2 = ((bf16[32,16,128]{2,1,0:T(8,128)(2,1)}), bf16[32,16,128]{2,1,0:T(8,128)(2,1)S(1)}, u32[]{:S(2)}, u32[]{:S(2)}) async-start(bf16[32,16,128]{2,1,0:T(8,128)(2,1)} %broadcast_in_dim.176), calls=%async_computation.2 | async-start | bytes 262144 | tf_op jit(solution)/shard_map/all_to_all | solution.py:18
  158.1 14.7 %all-to-all-start.3 = ((bf16[32,16,128]{2,1,0:T(8,128)(2,1)}), bf16[32,16,128]{2,1,0:T(8,128)(2,1)S(1)}, u32[]{:S(2)}, u32[]{:S(2)}) async-start(bf16[32,16,128]{2,1,0:T(8,128)(2,1)} %copy.80), calls=%async_computation.3 | async-start | bytes 262144 | tf_op jit(solution)/shard_map/all_to_all | solution.py:18
  173.3 31.2 %copy-start.5 = (bf16[1,1536]{1,0:T(2,128)(2,1)S(1)}, bf16[1,1536]{1,0:T(2,128)(2,1)}, u32[]{:S(2)}) copy-start(bf16[1,1536]{1,0:T(2,128)(2,1)} %param.18) | copy-start | bytes 9220
  173.3 31.2 %copy-start = (bf16[63,1536]{1,0:T(8,128)(2,1)S(1)}, bf16[63,1536]{1,0:T(8,128)(2,1)}, u32[]{:S(2)}) copy-start(bf16[63,1536]{1,0:T(8,128)(2,1)} %param.25) | copy-start | bytes 580612
  173.4 31.4 %copy-start.2 = (f32[1536]{0:T(1024)S(1)}, f32[1536]{0:T(1024)}, u32[]{:S(2)}) copy-start(f32[1536]{0:T(1024)} %param.28) | copy-start | bytes 18436
  177.9 14.4 %all-to-all-start.4 = ((bf16[32,12,128]{2,1,0:T(8,128)(2,1)}), bf16[32,12,128]{2,1,0:T(8,128)(2,1)S(1)}, u32[]{:S(2)}, u32[]{:S(2)}) async-start(bf16[32,12,128]{2,1,0:T(8,128)(2,1)} %broadcast_select_fusion), calls=%async_computation.4 | async-start | bytes 262144 | tf_op jit(solution)/shard_map/all_to_all | solution.py:18
  193.1 11.3 %all-to-all-start.5 = ((bf16[16,12,128]{2,1,0:T(8,128)(2,1)}), bf16[16,12,128]{2,1,0:T(8,128)(2,1)S(1)}, u32[]{:S(2)}, u32[]{:S(2)}) async-start(bf16[16,12,128]{2,1,0:T(8,128)(2,1)} %reshape.219), calls=%async_computation.5 | async-start | bytes 131072 | tf_op jit(solution)/shard_map/all_to_all | solution.py:18
  260.0 5.7 %copy-start.4 = (f32[64,4]{0,1:T(4,128)S(1)}, f32[64,4]{0,1:T(4,128)}, u32[]{:S(2)}) copy-start(f32[64,4]{0,1:T(4,128)} %param.27) | copy-start | bytes 3076
  260.0 44.4 %all-to-all-start.7 = ((bf16[32,16,1536]{2,1,0:T(8,128)(2,1)}), bf16[32,16,1536]{2,1,0:T(8,128)(2,1)S(1)}, u32[]{:S(2)}, u32[]{:S(2)}) async-start(bf16[32,16,1536]{2,1,0:T(8,128)(2,1)} %bitcast.24), calls=%async_computation.7 | async-start | bytes 3145728 | tf_op jit(solution)/shard_map/all_to_all | solution.py:18
  305.7 0.7 copy-start.1
Sparse Core Ops, SparseCore 0:
  11.2 91.8 all-gather.2
  105.2 55.1 all-gather.4
where the time goes:
time: 314 us; the launch traced here: 313 us
  waiting for transfers between devices  171 us (54%)
  blocking collectives  60.8 us (19%)
  starting transfers between devices  33 us (11%)
  between operations  19 us (6%)
  matrix products  18.5 us (6%)
  other arithmetic  5.56 us (2%)
  local copies, waits for them, and re-layouts  4.87 us (2%)
    all_gather x1, waiting for transfers between devices, on_device(): out_rows = lax.all_gather(w_out.T, 'tp', axis=0, tiled=True)  93.1 us
    all_to_all x6, waiting for transfers between devices, swap(): lax.all_to_all(blocks, axis_name, split_axis=0, concat_axis=0, tiled=True)  77.6 us
    all_to_all x2, blocking collectives, swap(): lax.all_to_all(blocks, axis_name, split_axis=0, concat_axis=0, tiled=True)  60.8 us
    all_to_all x6, starting transfers between devices, swap(): lax.all_to_all(blocks, axis_name, split_axis=0, concat_axis=0, tiled=True)  33 us
    dot_general x2, matrix products, contract_rows(): lax.dot_general(left_rows, unit_rows, (((1,), (1,)), ((), ())), preferred...  6.79 us
    dot_general x1, matrix products, expert_units(): return jnp.dot(active, units[2], preferred_element_type=F32).astype(BF16)  6.77 us
  transfers between devices with their start and end apart: 8, of which 7 were waited for; matrix products, arithmetic and copies ran while one was open for 5% of the time, Pallas kernels for 0%

commit v1 on v0

--- a/solution.py
+++ b/solution.py
@@ -6,6 +6,18 @@
 HIGHEST = lax.Precision.HIGHEST
 F32 = jnp.float32
 BF16 = jnp.bfloat16
+
+
+def _manage_sections(q_in):
+    return jnp.concatenate(
+        lax.all_to_all(
+            jnp.stack([q_in for _ in range(lax.axis_size("tp"))]),
+            axis_name="tp",
+            split_axis=0,
+            concat_axis=0,
+        ),
+        axis=0,
+    )
 
 
 def contract_rows(left_rows, unit_rows):
@@ -75,7 +87,7 @@
     total_reqs = placing.shape[0]
     experts = tp_size * w_gate.shape[0]
     assert group_reqs == tp_size and experts == tp_size
-    out_rows = lax.all_gather(w_out.T, "tp", axis=0, tiled=True)
+    out_rows = _manage_sections(w_out.T)
     stacked = jnp.concatenate([w_gate, w_up, w_down], axis=0)
     stacked, _ = lax.optimization_barrier((stacked, out_rows))
     units = lax.all_gather(stacked, "dp", axis=1, tiled=True)

time: 314 us -> 341 us (1.086)
  starting transfers between devices: 33 us -> 47.7 us
  waiting for transfers between devices: 171 us -> 185 us
  local copies, waits for them, and re-layouts: 4.87 us -> 8.45 us
    all_to_all x0 -> x1, waiting for transfers between devices: none -> 107 us  [_manage_sections(): lax.all_to_all(jnp.stack([q_in for _ in range(lax.axis_size('tp'))]), axi...]
    all_gather x1 -> x0, waiting for transfers between devices: 93.1 us -> none  [on_device(): out_rows = lax.all_gather(w_out.T, 'tp', axis=0, tiled=True)]
    all_to_all x0 -> x1, starting transfers between devices: none -> 10.5 us  [_manage_sections(): lax.all_to_all(jnp.stack([q_in for _ in range(lax.axis_size('tp'))]), axi...]
    all_to_all x6, starting transfers between devices: 33 us -> 37.1 us  [swap(): lax.all_to_all(blocks, axis_name, split_axis=0, concat_axis=0, tiled=True)]
    another operation x0 -> x1, local copies, waits for them, and re-layouts: none -> 3.56 us  [_manage_sections(): jnp.stack([q_in for _ in range(lax.axis_size('tp'))])]
  transfers between devices with their start and end apart: 8 -> 8, of which waited for: 7 -> 7; matrix products, arithmetic and copies ran while one was open for 5% -> 4% of each run, Pallas kernels for 0% -> 0%
where the time goes in v1:
time: 341 us; the launch traced here: 340 us
  waiting for transfers between devices  185 us (54%)
  blocking collectives  57.8 us (17%)
  starting transfers between devices  47.7 us (14%)
  between operations  19.1 us (6%)
  matrix products  18.5 us (5%)
  local copies, waits for them, and re-layouts  8.45 us (2%)
  other arithmetic  3.72 us (1%)
    all_to_all x1, waiting for transfers between devices, _manage_sections(): lax.all_to_all(jnp.stack([q_in for _ in range(lax.axis_size('tp'))]), axi...  107 us
    all_to_all x6, waiting for transfers between devices, swap(): lax.all_to_all(blocks, axis_name, split_axis=0, concat_axis=0, tiled=True)  77.5 us
    all_to_all x2, blocking collectives, swap(): lax.all_to_all(blocks, axis_name, split_axis=0, concat_axis=0, tiled=True)  57.8 us
    all_to_all x6, starting transfers between devices, swap(): lax.all_to_all(blocks, axis_name, split_axis=0, concat_axis=0, tiled=True)  37.1 us
    all_to_all x1, starting transfers between devices, _manage_sections(): lax.all_to_all(jnp.stack([q_in for _ in range(lax.axis_size('tp'))]), axi...  10.5 us
  transfers between devices with their start and end apart: 8, of which 7 were waited for; matrix products, arithmetic and copies ran while one was open for 4% of the time, Pallas kernels for 0%

profile of v1, /device:TPU:2, one launch (start us, length us, event | category | flops | bytes accessed | tf_op | source)
XLA Modules:
  0.0 339.8 jit_solution(2811960859565092823)
XLA Ops:
  7.2 3.6 %stack.2 = bf16[32,48,1536]{2,1,0:T(8,128)(2,1)} broadcast(bf16[48,1536]{1,0:T(8,128)(2,1)} %bitcast.101), dimensions={1,2} | broadcast | bytes 4866048 | tf_op jit(solution)/shard_map/stack | solution.py:14
  10.7 10.5 %all-to-all-start.4 = ((bf16[32,48,1536]{2,1,0:T(8,128)(2,1)}), bf16[32,48,1536]{2,1,0:T(8,128)(2,1)}, u32[]{:S(2)}, u32[]{:S(2)}) async-start(bf16[32,48,1536]{2,1,0:T(8,128)(2,1)} %stack.2), calls=%async_computation.4 | async-start | bytes 9437184 | tf_op jit(solution)/shard_map/all_to_all | solution.py:13
  21.4 0.8 pad_maximum_fusion
  22.2 107.1 %all-to-all-done.4 = bf16[32,48,1536]{2,1,0:T(8,128)(2,1)} async-done(((bf16[32,48,1536]{2,1,0:T(8,128)(2,1)}), bf16[32,48,1536]{2,1,0:T(8,128)(2,1)}, u32[]{:S(2)}, u32[]{:S(2)}) %all-to-all-start.4) | async-done | bytes 4718624 | tf_op jit(solution)/shard_map/all_to_all | solution.py:13
  129.5 13.0 %all_to_all.45 = bf16[32,1,128]{2,1,0:T(2,128)(2,1)S(1)} all-to-all(bf16[32,1,128]{2,1,0:T(2,128)(2,1)S(1)} %copy.71), channel_id=1, replica_groups=mesh['dp'=16,'tp'=32] {'tp'}, dimensions={0} | all-to-all | bytes 16384 | tf_op jit(solution)/shard_map/all_to_all | solution.py:30
  143.1 11.7 %all-to-all-start.1 = ((bf16[16,32,128]{2,1,0:T(8,128)(2,1)}), bf16[16,32,128]{2,1,0:T(8,128)(2,1)S(1)}, u32[]{:S(2)}, u32[]{:S(2)}) async-start(bf16[16,32,128]{2,1,0:T(8,128)(2,1)} %broadcast_in_dim.175), calls=%async_computation.1 | async-start | bytes 262144 | tf_op jit(solution)/shard_map/all_to_all | solution.py:30
  155.1 10.5 %all-to-all-done.1 = bf16[16,32,128]{2,1,0:T(8,128)(2,1)S(1)} async-done(((bf16[16,32,128]{2,1,0:T(8,128)(2,1)}), bf16[16,32,128]{2,1,0:T(8,128)(2,1)S(1)}, u32[]{:S(2)}, u32[]{:S(2)}) %all-to-all-start.1) | async-done | bytes 131104 | tf_op jit(solution)/shard_map/all_to_all | solution.py:30
  166.4 5.0 %all-to-all-start.2 = ((bf16[32,16,128]{2,1,0:T(8,128)(2,1)}), bf16[32,16,128]{2,1,0:T(8,128)(2,1)S(1)}, u32[]{:S(2)}, u32[]{:S(2)}) async-start(bf16[32,16,128]{2,1,0:T(8,128)(2,1)} %broadcast_in_dim.176), calls=%async_computation.2 | async-start | bytes 262144 | tf_op jit(solution)/shard_map/all_to_all | solution.py:30
  174.2 6.6 %all-to-all-done.2 = bf16[32,16,128]{2,1,0:T(8,128)(2,1)S(1)} async-done(((bf16[32,16,128]{2,1,0:T(8,128)(2,1)}), bf16[32,16,128]{2,1,0:T(8,128)(2,1)S(1)}, u32[]{:S(2)}, u32[]{:S(2)}) %all-to-all-start.2) | async-done | bytes 131104 | tf_op jit(solution)/shard_map/all_to_all | solution.py:30
  180.9 1.1 fusion.76
  182.8 1.3 convolution_convert_fusion.3
  184.9 5.7 %all-to-all-start.3 = ((bf16[32,16,128]{2,1,0:T(8,128)(2,1)}), bf16[32,16,128]{2,1,0:T(8,128)(2,1)S(1)}, u32[]{:S(2)}, u32[]{:S(2)}) async-start(bf16[32,16,128]{2,1,0:T(8,128)(2,1)} %copy.80), calls=%async_computation.3 | async-start | bytes 262144 | tf_op jit(solution)/shard_map/all_to_all | solution.py:30
  190.8 8.8 %all-to-all-done.3 = bf16[32,16,128]{2,1,0:T(8,128)(2,1)S(1)} async-done(((bf16[32,16,128]{2,1,0:T(8,128)(2,1)}), bf16[32,16,128]{2,1,0:T(8,128)(2,1)S(1)}, u32[]{:S(2)}, u32[]{:S(2)}) %all-to-all-start.3) | async-done | bytes 131104 | tf_op jit(solution)/shard_map/all_to_all | solution.py:30
  200.1 3.7 %convolution_reduce_fusion.1 = bf16[1536]{0:T(1024)(128)(2,1)S(1)} fusion(bf16[1536,1]{0,1:T(2,128)(2,1)S(1)} %reshape.241, bf16[1536,1536]{1,0:T(8,128)(2,1)} %bitcast.16), kind=kOutput, calls=%fused_computation.21 | convolution fusion | flops 4718592 | bytes 4724736 | tf_op jit(solution)/shard_map/dot_general | solution.py:24
  203.8 0.8 broadcast_select_fusion
  204.6 5.4 %all-to-all-start.5 = ((bf16[32,12,128]{2,1,0:T(8,128)(2,1)}), bf16[32,12,128]{2,1,0:T(8,128)(2,1)S(1)}, u32[]{:S(2)}, u32[]{:S(2)}) async-start(bf16[32,12,128]{2,1,0:T(8,128)(2,1)} %broadcast_select_fusion), calls=%async_computation.5 | async-start | bytes 262144 | tf_op jit(solution)/shard_map/all_to_all | solution.py:30
  210.1 8.8 %all-to-all-done.5 = bf16[32,12,128]{2,1,0:T(8,128)(2,1)S(1)} async-done(((bf16[32,12,128]{2,1,0:T(8,128)(2,1)}), bf16[32,12,128]{2,1,0:T(8,128)(2,1)S(1)}, u32[]{:S(2)}, u32[]{:S(2)}) %all-to-all-start.5) | async-done | bytes 98336 | tf_op jit(solution)/shard_map/all_to_all | solution.py:30
  219.8 3.5 %all-to-all-start.6 = ((bf16[16,12,128]{2,1,0:T(8,128)(2,1)}), bf16[16,12,128]{2,1,0:T(8,128)(2,1)S(1)}, u32[]{:S(2)}, u32[]{:S(2)}) async-start(bf16[16,12,128]{2,1,0:T(8,128)(2,1)} %reshape.235), calls=%async_computation.6 | async-start | bytes 131072 | tf_op jit(solution)/shard_map/all_to_all | solution.py:30
  226.8 4.3 %all-to-all-done.6 = bf16[16,12,128]{2,1,0:T(8,128)(2,1)S(1)} async-done(((bf16[16,12,128]{2,1,0:T(8,128)(2,1)}), bf16[16,12,128]{2,1,0:T(8,128)(2,1)S(1)}, u32[]{:S(2)}, u32[]{:S(2)}) %all-to-all-start.6) | async-done | bytes 49184 | tf_op jit(solution)/shard_map/all_to_all | solution.py:30
  232.1 44.8 %all_to_all.46 = bf16[32,16,1536]{2,1,0:T(8,128)(2,1)S(1)} all-to-all(bf16[32,16,1536]{2,1,0:T(8,128)(2,1)S(1)} %bitcast.92), channel_id=1, replica_groups=mesh['dp'=16,'tp'=32] {'tp'}, dimensions={0} | all-to-all | bytes 3145728 | tf_op jit(solution)/shard_map/all_to_all | solution.py:30
  276.9 3.1 fusion
  280.0 6.8 %convolution_convert_fusion = bf16[512,1536]{1,0:T(8,128)(2,1)} fusion(bf16[3,768,1536]{2,1,0:T(8,128)(2,1)} %all-gather.2.cloned.1.call-done, f32[512,768]{1,0:T(8,128)S(1)} %fusion, bf16[512,1536]{1,0:T(8,128)(2,1)S(1)} %bitcast.94), kind=kOutput, calls=%fused_computation | convolution fusion | flops 2417885184 | bytes 9437184 | tf_op jit(solution)/shard_map/dot_general | solution.py:58
  286.7 5.7 %all-to-all-start.8 = ((bf16[32,16,1536]{2,1,0:T(8,128)(2,1)}), bf16[32,16,1536]{2,1,0:T(8,128)(2,1)S(1)}, u32[]{:S(2)}, u32[]{:S(2)}) async-start(bf16[32,16,1536]{2,1,0:T(8,128)(2,1)} %bitcast.25), calls=%async_computation.8 | async-start | bytes 3145728 | tf_op jit(solution)/shard_map/all_to_all | solution.py:30
  292.5 38.4 %all-to-all-done.8 = bf16[32,16,1536]{2,1,0:T(8,128)(2,1)S(1)} async-done(((bf16[32,16,1536]{2,1,0:T(8,128)(2,1)}), bf16[32,16,1536]{2,1,0:T(8,128)(2,1)S(1)}, u32[]{:S(2)}, u32[]{:S(2)}) %all-to-all-start.8) | async-done | bytes 1572896 | tf_op jit(solution)/shard_map/all_to_all | solution.py:30
  (99 shorter events, 9.6 us)
Async XLA Ops:
  10.7 10.6 %copy-start.2 = (bf16[1,48,1536]{2,1,0:T(8,128)(2,1)S(1)}, bf16[1,48,1536]{2,1,0:T(8,128)(2,1)}, u32[]{:S(2)}) copy-start(bf16[1,48,1536]{2,1,0:T(8,128)(2,1)} %param.31) | copy-start | bytes 442372
  10.7 10.7 %copy-start.3 = (bf16[1,48,1536]{2,1,0:T(8,128)(2,1)S(1)}, bf16[1,48,1536]{2,1,0:T(8,128)(2,1)}, u32[]{:S(2)}) copy-start(bf16[1,48,1536]{2,1,0:T(8,128)(2,1)} %param.30) | copy-start | bytes 442372
  10.7 10.7 %copy-start.4 = (bf16[1,48,1536]{2,1,0:T(8,128)(2,1)S(1)}, bf16[1,48,1536]{2,1,0:T(8,128)(2,1)}, u32[]{:S(2)}) copy-start(bf16[1,48,1536]{2,1,0:T(8,128)(2,1)} %param.29) | copy-start | bytes 442372
  10.7 118.6 %copy-start.8 = (bf16[1,1536]{1,0:T(2,128)(2,1)S(1)}, bf16[1,1536]{1,0:T(2,128)(2,1)}, u32[]{:S(2)}) copy-start(bf16[1,1536]{1,0:T(2,128)(2,1)} %param.16) | copy-start | bytes 9220
  10.7 118.6 %copy-start.11 = (bf16[1,512]{1,0:T(2,128)(2,1)S(1)}, bf16[1,512]{1,0:T(2,128)(2,1)}, u32[]{:S(2)}) copy-start(bf16[1,512]{1,0:T(2,128)(2,1)} %param.17) | copy-start | bytes 3076
  10.7 118.6 %all-to-all-start.4 = ((bf16[32,48,1536]{2,1,0:T(8,128)(2,1)}), bf16[32,48,1536]{2,1,0:T(8,128)(2,1)}, u32[]{:S(2)}, u32[]{:S(2)}) async-start(bf16[32,48,1536]{2,1,0:T(8,128)(2,1)} %stack.2), calls=%async_computation.4 | async-start | bytes 9437184 | tf_op jit(solution)/shard_map/all_to_all | solution.py:13
  21.3 133.6 %copy-start.10 = (s32[512]{0:T(512)S(1)}, s32[512]{0:T(512)}, u32[]{:S(2)}) copy-start(s32[512]{0:T(512)} %param.19) | copy-start | bytes 6148
  21.3 133.8 %copy-start.6 = (s32[64,4]{0,1:T(4,128)S(1)}, s32[64,4]{0,1:T(4,128)}, u32[]{:S(2)}) copy-start(s32[64,4]{0,1:T(4,128)} %param.26) | copy-start | bytes 3076
  21.3 152.8 %copy-start.12 = (s32[32]{0:T(128)S(1)}, s32[32]{0:T(128)}, u32[]{:S(2)}) copy-start(s32[32]{0:T(128)} %param.20) | copy-start | bytes 388
  21.3 152.8 %copy-start.13 = (s32[32]{0:T(128)S(1)}, s32[32]{0:T(128)}, u32[]{:S(2)}) copy-start(s32[32]{0:T(128)} %param.21) | copy-start | bytes 388
  21.3 159.6 %copy-start.14 = (bf16[32,2,64,128]{3,2,1,0:T(8,128)(2,1)S(1)}, bf16[32,2,64,128]{3,2,1,0:T(8,128)(2,1)}, u32[]{:S(2)}) copy-start(bf16[32,2,64,128]{3,2,1,0:T(8,128)(2,1)} %param.22) | copy-start | bytes 3145732
  21.3 255.6 %all-gather.2.cloned.1.call-start = ((), (), s32[]{:S(2)}) async-start(), calls=%async_computation.9 | async-start | bytes 7520256 | tf_op jit(solution)/shard_map/all_gather | solution.py:93
  143.1 22.4 %all-to-all-start.1 = ((bf16[16,32,128]{2,1,0:T(8,128)(2,1)}), bf16[16,32,128]{2,1,0:T(8,128)(2,1)S(1)}, u32[]{:S(2)}, u32[]{:S(2)}) async-start(bf16[16,32,128]{2,1,0:T(8,128)(2,1)} %broadcast_in_dim.175), calls=%async_computation.1 | async-start | bytes 262144 | tf_op jit(solution)/shard_map/all_to_all | solution.py:30
  166.4 14.4 %all-to-all-start.2 = ((bf16[32,16,128]{2,1,0:T(8,128)(2,1)}), bf16[32,16,128]{2,1,0:T(8,128)(2,1)S(1)}, u32[]{:S(2)}, u32[]{:S(2)}) async-start(bf16[32,16,128]{2,1,0:T(8,128)(2,1)} %broadcast_in_dim.176), calls=%async_computation.2 | async-start | bytes 262144 | tf_op jit(solution)/shard_map/all_to_all | solution.py:30
  180.8 2.0 copy-start.15
  184.9 14.7 %all-to-all-start.3 = ((bf16[32,16,128]{2,1,0:T(8,128)(2,1)}), bf16[32,16,128]{2,1,0:T(8,128)(2,1)S(1)}, u32[]{:S(2)}, u32[]{:S(2)}) async-start(bf16[32,16,128]{2,1,0:T(8,128)(2,1)} %copy.80), calls=%async_computation.3 | async-start | bytes 262144 | tf_op jit(solution)/shard_map/all_to_all | solution.py:30
  200.1 31.1 %copy-start.9 = (bf16[1,1536]{1,0:T(2,128)(2,1)S(1)}, bf16[1,1536]{1,0:T(2,128)(2,1)}, u32[]{:S(2)}) copy-start(bf16[1,1536]{1,0:T(2,128)(2,1)} %param.18) | copy-start | bytes 9220
  200.1 31.1 %copy-start = (bf16[63,1536]{1,0:T(8,128)(2,1)S(1)}, bf16[63,1536]{1,0:T(8,128)(2,1)}, u32[]{:S(2)}) copy-start(bf16[63,1536]{1,0:T(8,128)(2,1)} %param.25) | copy-start | bytes 580612
  200.1 31.3 %copy-start.5 = (f32[1536]{0:T(1024)S(1)}, f32[1536]{0:T(1024)}, u32[]{:S(2)}) copy-start(f32[1536]{0:T(1024)} %param.28) | copy-start | bytes 18436
  204.6 14.3 %all-to-all-start.5 = ((bf16[32,12,128]{2,1,0:T(8,128)(2,1)}), bf16[32,12,128]{2,1,0:T(8,128)(2,1)S(1)}, u32[]{:S(2)}, u32[]{:S(2)}) async-start(bf16[32,12,128]{2,1,0:T(8,128)(2,1)} %broadcast_select_fusion), calls=%async_computation.5 | async-start | bytes 262144 | tf_op jit(solution)/shard_map/all_to_all | solution.py:30
  219.8 11.3 %all-to-all-start.6 = ((bf16[16,12,128]{2,1,0:T(8,128)(2,1)}), bf16[16,12,128]{2,1,0:T(8,128)(2,1)S(1)}, u32[]{:S(2)}, u32[]{:S(2)}) async-start(bf16[16,12,128]{2,1,0:T(8,128)(2,1)} %reshape.235), calls=%async_computation.6 | async-start | bytes 131072 | tf_op jit(solution)/shard_map/all_to_all | solution.py:30
  286.7 5.7 %copy-start.7 = (f32[64,4]{0,1:T(4,128)S(1)}, f32[64,4]{0,1:T(4,128)}, u32[]{:S(2)}) copy-start(f32[64,4]{0,1:T(4,128)} %param.27) | copy-start | bytes 3076
  286.7 44.2 %all-to-all-start.8 = ((bf16[32,16,1536]{2,1,0:T(8,128)(2,1)}), bf16[32,16,1536]{2,1,0:T(8,128)(2,1)S(1)}, u32[]{:S(2)}, u32[]{:S(2)}) async-start(bf16[32,16,1536]{2,1,0:T(8,128)(2,1)} %bitcast.25), calls=%async_computation.8 | async-start | bytes 3145728 | tf_op jit(solution)/shard_map/all_to_all | solution.py:30
  332.3 0.7 copy-start.1
Sparse Core Ops, SparseCore 0:
  129.5 56.3 all-gather.1
